TPU v7x, 128 devices: a whole 4x4x4 slice. The times are simulated.
128 devices in a mesh: period: 16 (over x, y), region: 8 (over z, core).
Axes of the slice: x: 4, y: 4, z: 4, core: 2. Of those that a mesh axis runs over, the one named last changes fastest.
Arguments:
- transition: float32 [128, 256, 128, 128], P('region', 'period'), may hold values from -0.05 to 1, as said below
- forcing: float32 [128, 256, 128], P('region', 'period'), may hold values from -0.8 to 0.8
- terminal: float32 [128, 128], P('region'), may hold values from -6 to 6
- partners: int32 [8, 128, 8], replicated, may hold values from 0 to 127
- shares: float32 [8, 128, 8], replicated, may hold values from 0.02 to 0.2
Outputs:
- costate: float32 [128, 256, 128], P('region', 'period')
- clearing: float32 [128, 256, 128], P(None, ('period', 'region'))
Inputs may be any that keep to these rules, and one draw needn't show every extreme that they name: The diagonal entries of each transition block lie from 0.54 to 1.0 and the off-diagonal entries are at most 0.05 in magnitude. `partners`: entries may repeat.
All inputs are finite; a program needn't handle non-finite values.
Results may differ from a plain program's by a relative error of at most 0.00013.
Values sent between devices are 32-bit elements; how exact they have to be, the bound alone decides.
A program may use at most 128 MiB of HBM per device.

v0:
```python
import jax
import jax.numpy as jnp
from jax import lax
from jax.sharding import PartitionSpec as P

BLOCKS = 8


def prefix(value, axis, join, neutral):
    count, mine = (lax.axis_size(axis), lax.axis_index(axis))
    pieces = jax.tree.map(lambda part: lax.all_gather(part, axis), value)
    pieces = jax.tree.map(lambda part: part[::-1], pieces)
    mine = count - 1 - mine
    so_far = jax.tree.map(
        lambda part, zero: jnp.full_like(part, 0) + jnp.asarray(zero, part.dtype), value, neutral
    )

    def step(position, so_far):
        longer = join(so_far, jax.tree.map(lambda part: part[position], pieces))
        return jax.tree.map(lambda new, old: jnp.where(position < mine, new, old), longer, so_far)

    return lax.fori_loop(0, count - 1, step, so_far)


def apply_map(matrix, vector):
    return jnp.einsum("rij,rj->ri", matrix, vector, precision=lax.Precision.HIGHEST)


def combine_maps(earlier, later):
    mat_early, vec_early = earlier
    mat_late, vec_late = later
    merged = jnp.einsum("rij,rjk->rik", mat_late, mat_early, precision=lax.Precision.HIGHEST)
    return (merged, apply_map(mat_late, vec_early) + vec_late)


def shards(transition, forcing, terminal, partners, shares):
    rows, per, sec = forcing.shape
    eye = jnp.eye(sec, dtype=jnp.float32)
    start_mat = jnp.broadcast_to(eye, (rows, sec, sec))
    start_vec = jnp.zeros((rows, sec), jnp.float32)

    def compose(step, carry):
        matrix, vector = carry
        when = per - 1 - step
        block = lax.dynamic_index_in_dim(transition, when, 1, keepdims=False)
        source = lax.dynamic_index_in_dim(forcing, when, 1, keepdims=False)
        matrix = jnp.einsum("rij,rjk->rik", block, matrix, precision=lax.Precision.HIGHEST)
        return (matrix, apply_map(block, vector) + source)

    block_mat, block_vec = lax.fori_loop(0, per, compose, (start_mat, start_vec))
    far_mat, far_vec = prefix(
        (block_mat, block_vec), "period", combine_maps, (start_mat, start_vec)
    )
    incoming = apply_map(far_mat, terminal) + far_vec

    def backward(step, carry):
        state, stored = carry
        when = per - 1 - step
        block = lax.dynamic_index_in_dim(transition, when, 1, keepdims=False)
        source = lax.dynamic_index_in_dim(forcing, when, 1, keepdims=False)
        state = apply_map(block, state) + source
        stored = lax.dynamic_update_index_in_dim(stored, state, when, 1)
        return (state, stored)

    last_state, costate = lax.fori_loop(0, per, backward, (incoming, jnp.zeros_like(forcing)))
    moved = lax.all_to_all(costate, "region", split_axis=1, concat_axis=0, tiled=True)
    regions = moved.shape[0]
    match = partners[..., None] == jnp.arange(regions, dtype=jnp.int32)
    trade = jnp.sum(jnp.where(match, shares[..., None], jnp.float32(0.0)), axis=2)
    flow = jnp.tanh(moved)
    blocked = flow.reshape(regions, moved.shape[1], BLOCKS, sec // BLOCKS)
    mixed = jnp.einsum("grq,qtgs->rtgs", trade, blocked, precision=lax.Precision.HIGHEST)
    clearing = (blocked - mixed).reshape(moved.shape)
    return (costate, clearing)


def solution(mesh):
    return jax.shard_map(
        shards,
        mesh=mesh,
        in_specs=(
            P("region", "period", None, None),
            P("region", "period", None),
            P("region", None),
            P(),
            P(),
        ),
        out_specs=(P("region", "period", None), P(None, ("period", "region"), None)),
        check_vma=False,
    )
```

profile of v0, /device:TPU:1, one launch (start us, length us, event | category | flops | bytes accessed | tf_op | source)
XLA Modules:
  0.0 405.2 jit_solution(11905498884728529681)
XLA Ops:
  7.4 102.5 %while.52 = (s32[]{:T(128)}, f32[16,128,128]{2,1,0:T(8,128)S(1)}, f32[16,128]{1,0:T(8,128)S(1)}, f32[16,16,128,128]{3,2,1,0:T(8,128)}, f32[16,16,128]{2,1,0:T(8,...) while((s32[]{:T(128)}, f32[16,128,128]{2,1,0:T(8,128)S(1)}, f32[16,128]{1,0:T(8,128)S(1)}, ...), condition=%wide.region_1.2_spmd.clone, body=%wide.region_0.1_spmd.clone.sunk | while | flops 405803008 | bytes 6365345 | solution.py:50
  7.4 3.0 fusion.55
  13.8 3.0 fusion.55
  20.2 3.0 fusion.55
  26.6 3.0 fusion.55
  33.0 3.0 fusion.55
  39.4 3.0 fusion.55
  45.8 3.0 fusion.55
  52.2 3.0 fusion.55
  58.7 3.0 fusion.55
  65.1 3.0 fusion.55
  71.5 3.0 fusion.55
  77.9 3.0 fusion.55
  84.3 3.0 fusion.55
  90.7 3.0 fusion.55
  97.1 3.0 fusion.55
  103.5 3.0 fusion.55
  110.9 20.5 %all-gather.1 = f32[256,128]{1,0:T(8,128)S(1)} all-gather(f32[16,128]{1,0:T(8,128)S(1)} %get-tuple-element.378), channel_id=3, replica_groups=mesh['period'=16,'region'=8] {'period'}, dimensions={0}, use_global_device_ids=true | all-gather | bytes 139264 | tf_op jit(solution)/shard_map/all_gather | solution.py:11
  131.8 93.9 %all-gather.4.cloned.1.call-done = f32[256,128,128]{2,1,0:T(8,128)} async-done(((f32[16,128,128]{2,1,0:T(8,128)}), f32[256,128,128]{2,1,0:T(8,128)}) %all-gather.4.cloned.1.call-update) | async-done | bytes 16777232 | tf_op jit(solution)/shard_map/all_gather | solution.py:11
  225.7 11.6 %rev.6 = f32[16,16,128,128]{3,2,1,0:T(8,128)} reverse(f32[16,16,128,128]{3,2,1,0:T(8,128)} %bitcast.113), dimensions={0} | reverse | bytes 33554432 | tf_op jit(solution)/shard_map/rev | solution.py:12
  237.5 82.9 %while.53 = (s32[]{:T(128)}, f32[16,128,128]{2,1,0:T(8,128)S(1)}, f32[16,128]{1,0:T(8,128)S(1)}, s32[]{:T(128)}, f32[16,16,128,128]{3,2,1,0:T(8,128)}, /*index=5*/f32[16,16,128]{2,1,0:T(8,128)S(1)}, s32[]{:T(128)}, s32[]{:T(128)}) while((s32[]{:T(128)}, f32[16,128,128]{2,1,0:T(8,128)S(1)}, f32[16,128]{1,0:T(8,128)S(1)}, s32[]{:T(128)}, ...), condition=%wide.region_3.4_spmd.clone, body=%wide.region_2.3_spmd.clone.sunk | while | flops 406069248 | bytes 7406703 | solution.py:22
  322.2 62.6 %while.51 = (s32[]{:T(128)}, f32[16,128]{1,0:T(8,128)S(1)}, f32[16,16,128]{2,1,0:T(8,128)S(1)}, f32[16,16,128,128]{3,2,1,0:T(8,128)}, f32[16,16,128]{2,1,0:T(8,1...) while((s32[]{:T(128)}, f32[16,128]{1,0:T(8,128)S(1)}, f32[16,16,128]{2,1,0:T(8,128)S(1)}, ...), condition=%wide.region_5.6_spmd, body=%wide.region_4.5_spmd.sunk | while | flops 3147782 | bytes 1122455 | solution.py:65
  330.0 3.0 fusion.49
  385.5 5.1 %all-to-all-start = ((f32[16,16,128]{2,0,1:T(8,128)}), f32[16,16,128]{2,0,1:T(8,128)S(1)}, u32[]{:S(2)}, u32[]{:S(2)}) async-start(f32[16,16,128]{2,0,1:T(8,128)} %copy.32), calls=%async_computation | async-start | bytes 262144 | tf_op jit(solution)/shard_map/all_to_all | solution.py:66
  (251 shorter events, 207.6 us)
Async XLA Ops:
  7.2 313.2 %copy-start = (f32[16,128]{1,0:T(8,128)S(1)}, f32[16,128]{1,0:T(8,128)}, u32[]{:S(2)}) copy-start(f32[16,128]{1,0:T(8,128)} %param.13) | copy-start | bytes 24580
  7.2 218.6 %all-gather.4.cloned.1.call-start = ((), (), s32[]{:S(2)}) async-start(), calls=%async_computation.1 | async-start | bytes 17825792 | tf_op jit(solution)/shard_map/all_gather | solution.py:11
  7.4 124.0 %copy-start.3 = (s32[8,128,8]{1,2,0:T(8,128)S(1)}, s32[8,128,8]{1,2,0:T(8,128)}, u32[]{:S(2)}) copy-start(s32[8,128,8]{1,2,0:T(8,128)} %param.14) | copy-start | bytes 98308
  7.4 124.2 %copy-start.4 = (f32[8,128,8]{1,2,0:T(8,128)S(1)}, f32[8,128,8]{1,2,0:T(8,128)}, u32[]{:S(2)}) copy-start(f32[8,128,8]{1,2,0:T(8,128)} %param.15) | copy-start | bytes 98308
  109.9 1.0 copy-start.1
  384.8 13.6 %copy-start.2 = (f32[16,16,128]{2,1,0:T(8,128)}, f32[16,16,128]{2,1,0:T(8,128)S(1)}, u32[]{:S(2)}) copy-start(f32[16,16,128]{2,1,0:T(8,128)S(1)} %get-tuple-element.465) | copy-start | bytes 393220
  385.5 10.4 %all-to-all-start = ((f32[16,16,128]{2,0,1:T(8,128)}), f32[16,16,128]{2,0,1:T(8,128)S(1)}, u32[]{:S(2)}, u32[]{:S(2)}) async-start(f32[16,16,128]{2,0,1:T(8,128)} %copy.32), calls=%async_computation | async-start | bytes 262144 | tf_op jit(solution)/shard_map/all_to_all | solution.py:66
Sparse Core Ops, SparseCore 0:
  111.0 114.7 all-gather.3
where the time goes:
time: 410 us; the launch traced here: 405 us
  matrix products  217 us (53%)
  waiting for transfers between devices  96.4 us (24%)
  local copies, waits for them, and re-layouts  46.7 us (11%)
  blocking collectives  20.5 us (5%)
  between operations  14.2 us (3%)
  starting transfers between devices  5.17 us (1%)
    dot_general x48, matrix products, apply_map(): jnp.einsum('rij,rj->ri', matrix, vector, precision=lax.Precision.HIGHEST)  141 us
    all_gather x1, waiting for transfers between devices, prefix(): pieces = jax.tree.map(lambda part: lax.all_gather(part, axis), value)  93.9 us
    dot_general x16, matrix products, compose(): jnp.einsum('rij,rjk->rik', block, matrix, precision=lax.Precision.HIGHEST)  38.9 us
    dot_general x15, matrix products, combine_maps(): jnp.einsum('rij,rjk->rik', mat_late, mat_early, precision=lax.Precision.H...  36.5 us
    all_gather x1, blocking collectives, prefix(): pieces = jax.tree.map(lambda part: lax.all_gather(part, axis), value)  20.5 us
    dynamic_slice x16, local copies, waits for them, and re-layouts, compose(): source = lax.dynamic_index_in_dim(forcing, when, 1, keepdims=False)  13.8 us
    dynamic_slice x16, local copies, waits for them, and re-layouts, backward(): source = lax.dynamic_index_in_dim(forcing, when, 1, keepdims=False)  13.8 us
    rev x2, local copies, waits for them, and re-layouts, prefix(): pieces = jax.tree.map(lambda part: part[::-1], pieces)  11.7 us
  transfers between devices with their start and end apart: 2, of which 2 were waited for; matrix products, arithmetic and copies ran while one was open for 1% of the time, Pallas kernels for 0%

commit v1 on v0

v1 whole, which is shorter than its diff:
```python
import functools

import jax
import jax.numpy as jnp
from jax import lax
from jax.experimental import pallas as pl
from jax.experimental.pallas import tpu as pltpu
from jax.sharding import PartitionSpec as P

BLOCKS = 8
BATCH = 4
NT = (((1,), (1,)), ((), ()))
NN = (((1,), (0,)), ((), ()))
F32 = jnp.float32
BF16 = jnp.bfloat16
MESH = pl.DeviceIdType.MESH


def split(x):
    high = x.astype(BF16)
    return high, (x - high.astype(F32)).astype(BF16)


def dot(left, right, dims):
    return lax.dot_general(left, right, dims, preferred_element_type=F32)


def kernel(
    nper,
    nreg,
    trans_hbm,
    force_hbm,
    term_hbm,
    part_hbm,
    share_hbm,
    costate_hbm,
    clear_hbm,
    maps,
    force,
    term,
    part,
    share,
    offsets,
    left,
    outgoing,
    incoming,
    edges,
    starts,
    costate,
    flow,
    traded,
    mixer,
    clear,
    load_sem,
    small_sem,
    map_send,
    map_recv,
    edge_send,
    edge_recv,
    flow_send,
    flow_recv,
    out_sem,
):
    rows, per, sec = force.shape
    here, zone = lax.axis_index("period"), lax.axis_index("region")
    batches = rows // BATCH
    chunk = per // 4
    share_t = per // nreg
    half = rows // 2

    def base_of(k):
        return lax.rem(lax.div(here, BATCH) + 1 + k, batches) * BATCH

    def load(k, c):
        where = (pl.ds(base_of(k), BATCH), pl.ds(per - chunk * (c + 1), chunk))
        return pltpu.make_async_copy(trans_hbm.at[where], maps.at[where], load_sem.at[k, c])

    small = [
        pltpu.make_async_copy(src, dst, small_sem.at[i])
        for i, (src, dst) in enumerate(
            [(force_hbm, force), (term_hbm, term), (part_hbm, part), (share_hbm, share)]
        )
    ]
    small[0].start()
    for k in range(batches):
        for c in range(4):
            load(k, c).start()
    for copy in small[1:]:
        copy.start()

    barrier = pltpu.get_barrier_semaphore()
    for step in range(1, nper):
        pl.semaphore_signal(
            barrier, inc=1, device_id=(lax.rem(here + step, nper), zone), device_id_type=MESH
        )
    for step in range(1, nreg):
        pl.semaphore_signal(
            barrier, inc=1, device_id=(here, lax.rem(zone + step, nreg)), device_id_type=MESH
        )

    square = (sec, sec)
    eye = lax.broadcasted_iota(jnp.int32, square, 0) == lax.broadcasted_iota(jnp.int32, square, 1)
    top = lax.broadcasted_iota(jnp.int32, (16, sec), 0) == 0

    def send_map(row):
        return pltpu.make_async_remote_copy(
            src_ref=outgoing.at[row],
            dst_ref=incoming.at[here],
            send_sem=map_send.at[row],
            recv_sem=map_recv.at[here],
            device_id=(row, zone),
            device_id_type=MESH,
        )

    def keep_map():
        return pltpu.make_async_copy(outgoing.at[here], incoming.at[here], map_recv.at[here])

    small[0].wait()

    def compose(k, carry):
        base = base_of(k)
        for c in range(4):
            load(k, c).wait()
            for inner in range(chunk):
                t = per - 1 - chunk * c - inner
                for i in range(BATCH):
                    row = base + i
                    block = maps[row, t]
                    source = force[row, t : t + 1]
                    if t == per - 1:
                        prod = block.T
                        offset = jnp.where(top, source, 0.0)
                    else:
                        diag = jnp.sum(jnp.where(eye, block, 0.0), axis=0, keepdims=True)
                        high, low = split(jnp.where(eye, 0.0, block))
                        held = left[i]
                        prod = dot(held, jnp.concatenate([high, high], 1), NT)
                        prod += dot(held[:, :sec], low, NT)
                        offset = prod[sec:] + offsets[row, t + 1 : t + 2] * diag + source
                        offset = jnp.where(top, offset, 0.0)
                        prod = prod[:sec] + maps[row, t + 1] * diag
                    maps[row, t] = prod
                    offsets[row, t : t + 1] = offset[:1]
                    if t > 0:
                        high, low = split(prod)
                        left[i, :sec, :sec] = high
                        left[i, :sec, sec:] = low
                        high, low = split(offset)
                        left[i, sec:, :sec] = high
                        left[i, sec:, sec:] = low
                    else:
                        outgoing[row, :sec] = prod
                        outgoing[row, sec:] = offset[:8]

        @pl.when(k == 0)
        def _():
            pl.semaphore_wait(barrier, nper + nreg - 2)

        for i in range(BATCH):

            @pl.when((base + i != here) & (here != 0))
            def _():
                send_map(base + i).start()

            @pl.when((base + i == here) & (here != 0))
            def _():
                keep_map().start()

        return carry

    lax.fori_loop(0, batches, compose, 0)

    for copy in small[1:]:
        copy.wait()

    region = lax.broadcasted_iota(jnp.int32, square, 0)
    for g in range(BLOCKS):
        ids, amounts = part[g], share[g]
        trade = jnp.zeros(square, F32)
        for j in range(ids.shape[0]):
            trade += jnp.where(ids[j : j + 1] == region, amounts[j : j + 1], 0.0)
        high, low = split(trade.T)
        side = sec * (g % 2)
        mixer[g // 2, :sec, side : side + sec] = high
        mixer[g // 2, sec:, side : side + sec] = low

    def upright(vector):
        return jnp.sum(jnp.where(eye, vector, 0.0), axis=1, keepdims=True)

    def send_edge(p):
        return pltpu.make_async_remote_copy(
            src_ref=edges.at[p],
            dst_ref=starts.at[here],
            send_sem=edge_send.at[p],
            recv_sem=edge_recv.at[here],
            device_id=(p, zone),
            device_id_type=MESH,
        )

    def keep_edge():
        return pltpu.make_async_copy(edges.at[here], starts.at[here], edge_recv.at[here])

    def ship_edge(p):
        @pl.when(p != here)
        def _():
            send_edge(p).start()

        @pl.when(p == here)
        def _():
            keep_edge().start()

    state = term[pl.ds(here, 1), :]
    edges[nper - 1] = state

    def chain(step, state):
        p = nper - 1 - step

        @pl.when(p != here)
        def _():
            pltpu.make_async_remote_copy(
                src_ref=outgoing.at[p],
                dst_ref=incoming.at[p],
                send_sem=map_send.at[p],
                recv_sem=map_recv.at[p],
                device_id=(p, zone),
                device_id_type=MESH,
            ).wait_recv()

        @pl.when(p == here)
        def _():
            keep_map().wait()

        ship_edge(p)
        moved = incoming[p, :sec] * upright(state)
        state = jnp.sum(moved, axis=0, keepdims=True) + incoming[p, sec : sec + 1]
        edges[p - 1] = state
        return state

    lax.fori_loop(0, nper - 1, chain, state)
    ship_edge(0)

    def finish(i, carry):
        row = lax.rem(lax.div(here, half) * half + i, rows)

        @pl.when(row != here)
        def _():
            pltpu.make_async_remote_copy(
                src_ref=edges.at[row],
                dst_ref=starts.at[row],
                send_sem=edge_send.at[row],
                recv_sem=edge_recv.at[row],
                device_id=(row, zone),
                device_id_type=MESH,
            ).wait_recv()

        @pl.when(row == here)
        def _():
            keep_edge().wait()

        column = jnp.broadcast_to(upright(starts[row]), square)
        lines = [jnp.sum(maps[row, t] * column, axis=0, keepdims=True) for t in range(per)]
        value = jnp.concatenate(lines, 0) + offsets[row]
        costate[row] = value
        bent = jnp.tanh(value)
        for t in range(per):
            flow[t, pl.ds(row, 1), :] = bent[t : t + 1]
        return carry

    def send_flow(other, h):
        mine = pl.multiple_of(zone * rows + h * half, 8)
        return pltpu.make_async_remote_copy(
            src_ref=flow.at[pl.ds(other * share_t, share_t), pl.ds(h * half, half)],
            dst_ref=traded.at[:, pl.ds(mine, half)],
            send_sem=flow_send.at[other, h],
            recv_sem=flow_recv.at[zone, h],
            device_id=(here, other),
            device_id_type=MESH,
        )

    def keep_flow(h):
        mine = pl.multiple_of(zone * rows + h * half, 8)
        return pltpu.make_async_copy(
            flow.at[pl.ds(zone * share_t, share_t), pl.ds(h * half, half)],
            traded.at[:, pl.ds(mine, half)],
            flow_recv.at[zone, h],
        )

    def got_flow(other, h):
        theirs = pl.multiple_of(other * rows + h * half, 8)
        return pltpu.make_async_remote_copy(
            src_ref=flow.at[pl.ds(other * share_t, share_t), pl.ds(h * half, half)],
            dst_ref=traded.at[:, pl.ds(theirs, half)],
            send_sem=flow_send.at[other, h],
            recv_sem=flow_recv.at[other, h],
            device_id=(here, other),
            device_id_type=MESH,
        )

    for part_no in range(2):
        lax.fori_loop(part_no * half, (part_no + 1) * half, finish, 0)
        h = lax.rem(lax.div(here, half) + part_no, 2)
        for step in range(1, nreg):
            send_flow(lax.rem(zone + step, nreg), h).start()
        keep_flow(h).start()
    save = pltpu.make_async_copy(costate, costate_hbm, out_sem.at[0])
    save.start()

    for part_no in range(2):
        h = lax.rem(lax.div(here, half) + part_no, 2)
        for step in range(1, nreg):
            got_flow(lax.rem(zone + step, nreg), h).wait_recv()
        keep_flow(h).wait()

    width = share_t * sec
    whole = jnp.concatenate([traded[t] for t in range(share_t)], 1)
    high, low = split(whole)
    group = lax.div(
        lax.rem(lax.broadcasted_iota(jnp.int32, (1, width), 1), sec), sec // BLOCKS
    )
    mixed = jnp.zeros((sec, width), F32)
    for pair in range(BLOCKS // 2):
        masks = [group == 2 * pair, group == 2 * pair + 1]
        tall_high = jnp.concatenate([jnp.where(m, high, BF16(0)) for m in masks], 0)
        tall_low = jnp.concatenate([jnp.where(m, low, BF16(0)) for m in masks], 0)
        first = dot(mixer[pair], tall_high, NN)
        mixed += first[:sec] + first[sec:]
        mixed += dot(mixer[pair, :sec], tall_low, NN)
    result = whole - mixed
    for t in range(share_t):
        clear[t] = result[:, t * sec : (t + 1) * sec]
    done = pltpu.make_async_copy(clear, clear_hbm, out_sem.at[1])
    done.start()

    def drain(row, carry):
        @pl.when(row != here)
        def _():
            send_edge(row).wait_send()

        @pl.when((row != here) & (here != 0))
        def _():
            send_map(row).wait_send()

        return carry

    lax.fori_loop(0, rows, drain, 0)

    for step in range(1, nreg):
        for h in range(2):
            send_flow(lax.rem(zone + step, nreg), h).wait_send()
    save.wait()
    done.wait()


def shards(nper, nreg, transition, forcing, terminal, partners, shares):
    rows, per, sec = forcing.shape
    regions = partners.shape[1]
    share_t = per // nreg
    ids, amounts = jnp.swapaxes(partners, 1, 2), jnp.swapaxes(shares, 1, 2)
    anywhere = pl.BlockSpec(memory_space=pl.ANY)
    dma = pltpu.SemaphoreType.DMA
    costate, clearing = pl.pallas_call(
        functools.partial(kernel, nper, nreg),
        out_shape=(
            jax.ShapeDtypeStruct((rows, per, sec), F32),
            jax.ShapeDtypeStruct((share_t, regions, sec), F32),
        ),
        in_specs=[anywhere] * 5,
        out_specs=[anywhere] * 2,
        scratch_shapes=[
            pltpu.VMEM((rows, per, sec, sec), F32),
            pltpu.VMEM((rows, per, sec), F32),
            pltpu.VMEM((rows, sec), F32),
            pltpu.VMEM(ids.shape, jnp.int32),
            pltpu.VMEM(amounts.shape, F32),
            pltpu.VMEM((rows, per, sec), F32),
            pltpu.VMEM((BATCH, sec + 16, 2 * sec), BF16),
            pltpu.VMEM((rows, sec + 8, sec), F32),
            pltpu.VMEM((nper, sec + 8, sec), F32),
            pltpu.VMEM((nper, 1, sec), F32),
            pltpu.VMEM((rows, 1, sec), F32),
            pltpu.VMEM((rows, per, sec), F32),
            pltpu.VMEM((per, rows, sec), F32),
            pltpu.VMEM((share_t, regions, sec), F32),
            pltpu.VMEM((BLOCKS // 2, 2 * regions, 2 * regions), BF16),
            pltpu.VMEM((share_t, regions, sec), F32),
            dma((rows // BATCH, 4)),
            dma((4,)),
            dma((rows,)),
            dma((nper,)),
            dma((nper,)),
            dma((rows,)),
            dma((nreg, 2)),
            dma((nreg, 2)),
            dma((2,)),
        ],
        compiler_params=pltpu.CompilerParams(
            collective_id=0, has_side_effects=True, vmem_limit_bytes=60 * 2**20
        ),
        name="newton_step",
    )(transition, forcing, terminal, ids, amounts)
    return costate, jnp.swapaxes(clearing, 0, 1)


def solution(mesh):
    return jax.shard_map(
        functools.partial(shards, mesh.shape["period"], mesh.shape["region"]),
        mesh=mesh,
        in_specs=(
            P("region", "period", None, None),
            P("region", "period", None),
            P("region", None),
            P(),
            P(),
        ),
        out_specs=(P("region", "period", None), P(None, ("period", "region"), None)),
        check_vma=False,
    )
```

time: 410 us -> 45.9 us (0.11); the launches traced: 405 us -> 45.7 us
  matrix products: 217 us -> 0 us
  waiting for transfers between devices: 96.4 us -> 0 us
  local copies, waits for them, and re-layouts: 46.7 us -> 3.23 us
  Pallas kernels: 0 us -> 41.9 us
  blocking collectives: 20.5 us -> 0 us
  between operations: 14.2 us -> 0.64 us
  starting transfers between devices: 5.17 us -> 0 us
    dot_general x80 -> x0, matrix products: 217 us -> none  [the longest x48 141 us: apply_map(): jnp.einsum('rij,rj->ri', matrix, vector, precision=lax.Precision.HIGHEST)]
    all_gather x1 -> x0, waiting for transfers between devices: 93.9 us -> none  [prefix(): pieces = jax.tree.map(lambda part: lax.all_gather(part, axis), value)]
    pallas_call x0 -> x1, Pallas kernels: none -> 41.9 us  [shards(): pl.pallas_call(functools.partial(kernel, nper, nreg), out_shape=(jax.Shap...]
    dynamic_slice x32 -> x0, local copies, waits for them, and re-layouts: 27.7 us -> none  [the longest x16 13.8 us: compose(): source = lax.dynamic_index_in_dim(forcing, when, 1, keepdims=False)]
    all_gather x1 -> x0, blocking collectives: 20.5 us -> none  [prefix(): pieces = jax.tree.map(lambda part: lax.all_gather(part, axis), value)]
    rev x2 -> x0, local copies, waits for them, and re-layouts: 11.7 us -> none  [prefix(): pieces = jax.tree.map(lambda part: part[::-1], pieces)]
    all_to_all x1 -> x0, starting transfers between devices: 5.14 us -> none  [shards(): lax.all_to_all(costate, 'region', split_axis=1, concat_axis=0, tiled=True)]
  transfers between devices with their start and end apart: 2 -> 0, of which waited for: 2 -> 0; matrix products, arithmetic and copies ran while one was open for 1% -> 0% of each run, Pallas kernels for 0% -> 0%
where the time goes in v1:
time: 45.9 us; the launch traced here: 45.7 us
  Pallas kernels  41.9 us (91%)
  local copies, waits for them, and re-layouts  3.23 us (7%)
  between operations  0.64 us (1%)
    pallas_call x1, Pallas kernels, shards(): pl.pallas_call(functools.partial(kernel, nper, nreg), out_shape=(jax.Shap...  41.9 us
    unnamed x2, local copies, waits for them, and re-layouts  3.23 us

profile of v1, /device:TPU:1, one launch (start us, length us, event | category | flops | bytes accessed | tf_op | source)
XLA Modules:
  0.0 45.7 jit_solution(12175557685390858817)
XLA Ops:
  0.6 41.9 %newton_step.1 = (f32[16,16,128]{2,1,0:T(8,128)}, f32[2,128,128]{2,1,0:T(8,128)}) custom-call(f32[16,16,128,128]{3,2,1,0:T(8,128)} %trans_hbm.1, f32[16,16,128]{2,1,0:T(8,128)} %force_hbm.1, f32[16,128]{1,0:T(8,128)} %term_hbm.1, s32[8,8,128]{2,1,0:T(8,128)} %bitcast.4, f32[8,8,128]{2,1,0:T(8,128)} %bitcast.5), custom_call_target="tpu_custom_call" | custom-call | tf_op jit(solution)/shard_map/newton_step/pallas_call | solution.py:361
  42.5 1.7 %copy.7 = f32[128,2,128]{2,1,0:T(2,128)} copy(f32[128,2,128]{2,0,1:T(8,128)} %bitcast.3) | data formatting | bytes 262144
  44.2 1.6 %copy.9 = f32[16,16,128]{2,1,0:T(8,128)} copy(f32[16,16,128]{2,1,0:T(8,128)} %get-tuple-element.10) | data formatting | bytes 262144

commit v2 on v1

--- a/solution.py
+++ b/solution.py
@@ -41,7 +41,6 @@
     part,
     share,
     offsets,
-    left,
     outgoing,
     incoming,
     edges,
@@ -68,12 +67,22 @@
     share_t = per // nreg
     half = rows // 2
 
-    def base_of(k):
-        return lax.rem(lax.div(here, BATCH) + 1 + k, batches) * BATCH
-
-    def load(k, c):
-        where = (pl.ds(base_of(k), BATCH), pl.ds(per - chunk * (c + 1), chunk))
-        return pltpu.make_async_copy(trans_hbm.at[where], maps.at[where], load_sem.at[k, c])
+    def row_of(k, i):
+        skew = k + lax.div(k, 2) * (1 - 2 * lax.rem(k, 2))
+        along_x = lax.rem(lax.div(here, BATCH) + i, batches)
+        return along_x * BATCH + lax.rem(here + i + skew, BATCH)
+
+    def slot_of(row):
+        i = lax.rem(lax.div(row, BATCH) + batches - lax.div(here, BATCH), batches)
+        skew = lax.rem(row + 2 * BATCH - lax.rem(here, BATCH) - i, BATCH)
+        k = skew + lax.div(skew, 2) * (1 - 2 * lax.rem(skew, 2))
+        return k * BATCH + i
+
+    def load(k, c, i):
+        when = pl.ds(per - chunk * (c + 1), chunk)
+        return pltpu.make_async_copy(
+            trans_hbm.at[row_of(k, i), when], maps.at[k * BATCH + i, when], load_sem.at[k, c, i]
+        )
 
     small = [
         pltpu.make_async_copy(src, dst, small_sem.at[i])
@@ -84,7 +93,8 @@
     small[0].start()
     for k in range(batches):
         for c in range(4):
-            load(k, c).start()
+            for i in range(BATCH):
+                load(k, c, i).start()
     for copy in small[1:]:
         copy.start()
 
@@ -102,67 +112,68 @@
     eye = lax.broadcasted_iota(jnp.int32, square, 0) == lax.broadcasted_iota(jnp.int32, square, 1)
     top = lax.broadcasted_iota(jnp.int32, (16, sec), 0) == 0
 
-    def send_map(row):
+    def send_map(k, i):
+        row, slot = row_of(k, i), k * BATCH + i
         return pltpu.make_async_remote_copy(
-            src_ref=outgoing.at[row],
+            src_ref=outgoing.at[slot],
             dst_ref=incoming.at[here],
-            send_sem=map_send.at[row],
+            send_sem=map_send.at[slot],
             recv_sem=map_recv.at[here],
             device_id=(row, zone),
             device_id_type=MESH,
         )
 
     def keep_map():
-        return pltpu.make_async_copy(outgoing.at[here], incoming.at[here], map_recv.at[here])
+        return pltpu.make_async_copy(outgoing.at[0], incoming.at[here], map_recv.at[here])
 
     small[0].wait()
 
     def compose(k, carry):
-        base = base_of(k)
         for c in range(4):
-            load(k, c).wait()
+            for i in range(BATCH):
+                load(k, c, i).wait()
             for inner in range(chunk):
                 t = per - 1 - chunk * c - inner
                 for i in range(BATCH):
-                    row = base + i
-                    block = maps[row, t]
+                    row, slot = row_of(k, i), k * BATCH + i
+                    block = maps[slot, t]
                     source = force[row, t : t + 1]
                     if t == per - 1:
                         prod = block.T
-                        offset = jnp.where(top, source, 0.0)
+                        offset = jnp.broadcast_to(source, (8, sec))
                     else:
                         diag = jnp.sum(jnp.where(eye, block, 0.0), axis=0, keepdims=True)
                         high, low = split(jnp.where(eye, 0.0, block))
-                        held = left[i]
-                        prod = dot(held, jnp.concatenate([high, high], 1), NT)
-                        prod += dot(held[:, :sec], low, NT)
-                        offset = prod[sec:] + offsets[row, t + 1 : t + 2] * diag + source
-                        offset = jnp.where(top, offset, 0.0)
-                        prod = prod[:sec] + maps[row, t + 1] * diag
-                    maps[row, t] = prod
-                    offsets[row, t : t + 1] = offset[:1]
-                    if t > 0:
-                        high, low = split(prod)
-                        left[i, :sec, :sec] = high
-                        left[i, :sec, sec:] = low
-                        high, low = split(offset)
-                        left[i, sec:, :sec] = high
-                        left[i, sec:, sec:] = low
-                    else:
-                        outgoing[row, :sec] = prod
-                        outgoing[row, sec:] = offset[:8]
+                        late, late_offset = maps[slot, t + 1], offsets[slot, t + 1 : t + 2]
+                        late_high, late_low = split(late)
+                        tail_high, tail_low = split(jnp.where(top, late_offset, 0.0))
+                        tall_high = jnp.concatenate([late_high, tail_high], 0)
+                        tall_low = jnp.concatenate([late_low, tail_low], 0)
+                        prod = dot(
+                            jnp.concatenate([tall_high, tall_low, tall_high], 1),
+                            jnp.concatenate([high, high, low], 1),
+                            NT,
+                        )
+                        offset = prod[sec : sec + 8] + late_offset * diag + source
+                        prod = prod[:sec] + late * diag
+                    maps[slot, t] = prod
+                    offsets[slot, t : t + 1] = offset[:1]
+                    if t == 0:
+                        outgoing[slot, :sec] = prod
+                        outgoing[slot, sec:] = offset
 
         @pl.when(k == 0)
         def _():
             pl.semaphore_wait(barrier, nper + nreg - 2)
 
-        for i in range(BATCH):
-
-            @pl.when((base + i != here) & (here != 0))
-            def _():
-                send_map(base + i).start()
-
-            @pl.when((base + i == here) & (here != 0))
+        for i in (2, 1, 3, 0):
+            row = row_of(k, i)
+
+            @pl.when((row != here) & (here != 0))
+            def _(i=i):
+                send_map(k, i).start()
+
+            @pl.when((row == here) & (here != 0))
             def _():
                 keep_map().start()
 
@@ -241,6 +252,7 @@
 
     def finish(i, carry):
         row = lax.rem(lax.div(here, half) * half + i, rows)
+        slot = slot_of(row)
 
         @pl.when(row != here)
         def _():
@@ -258,8 +270,8 @@
             keep_edge().wait()
 
         column = jnp.broadcast_to(upright(starts[row]), square)
-        lines = [jnp.sum(maps[row, t] * column, axis=0, keepdims=True) for t in range(per)]
-        value = jnp.concatenate(lines, 0) + offsets[row]
+        lines = [jnp.sum(maps[slot, t] * column, axis=0, keepdims=True) for t in range(per)]
+        value = jnp.concatenate(lines, 0) + offsets[slot]
         costate[row] = value
         bent = jnp.tanh(value)
         for t in range(per):
@@ -336,9 +348,9 @@
         def _():
             send_edge(row).wait_send()
 
-        @pl.when((row != here) & (here != 0))
-        def _():
-            send_map(row).wait_send()
+        @pl.when((row > 0) & (here != 0))
+        def _():
+            send_map(lax.div(row, BATCH), lax.rem(row, BATCH)).wait_send()
 
         return carry
 
@@ -373,7 +385,6 @@
             pltpu.VMEM(ids.shape, jnp.int32),
             pltpu.VMEM(amounts.shape, F32),
             pltpu.VMEM((rows, per, sec), F32),
-            pltpu.VMEM((BATCH, sec + 16, 2 * sec), BF16),
             pltpu.VMEM((rows, sec + 8, sec), F32),
             pltpu.VMEM((nper, sec + 8, sec), F32),
             pltpu.VMEM((nper, 1, sec), F32),
@@ -383,7 +394,7 @@
             pltpu.VMEM((share_t, regions, sec), F32),
             pltpu.VMEM((BLOCKS // 2, 2 * regions, 2 * regions), BF16),
             pltpu.VMEM((share_t, regions, sec), F32),
-            dma((rows // BATCH, 4)),
+            dma((rows // BATCH, 4, BATCH)),
             dma((4,)),
             dma((rows,)),
             dma((nper,)),

time: 45.9 us -> 47.8 us (1.041)
  Pallas kernels: 41.9 us -> 43.8 us
    pallas_call x1, Pallas kernels: 41.9 us -> 43.8 us  [shards(): pl.pallas_call(functools.partial(kernel, nper, nreg), out_shape=(jax.Shap...]
where the time goes in v2:
time: 47.8 us; the launch traced here: 47.7 us
  Pallas kernels  43.8 us (92%)
  local copies, waits for them, and re-layouts  3.23 us (7%)
  between operations  0.64 us (1%)
    pallas_call x1, Pallas kernels, shards(): pl.pallas_call(functools.partial(kernel, nper, nreg), out_shape=(jax.Shap...  43.8 us
    unnamed x2, local copies, waits for them, and re-layouts  3.23 us

profile of v2, /device:TPU:1, one launch (start us, length us, event | category | flops | bytes accessed | tf_op | source)
XLA Modules:
  0.0 47.7 jit_solution(1927715310206884653)
XLA Ops:
  0.6 43.8 %newton_step.1 = (f32[16,16,128]{2,1,0:T(8,128)}, f32[2,128,128]{2,1,0:T(8,128)}) custom-call(f32[16,16,128,128]{3,2,1,0:T(8,128)} %trans_hbm.1, f32[16,16,128]{2,1,0:T(8,128)} %force_hbm.1, f32[16,128]{1,0:T(8,128)} %term_hbm.1, s32[8,8,128]{2,1,0:T(8,128)} %bitcast.4, f32[8,8,128]{2,1,0:T(8,128)} %bitcast.5), custom_call_target="tpu_custom_call" | custom-call | tf_op jit(solution)/shard_map/newton_step/pallas_call | solution.py:373
  44.4 1.7 %copy.7 = f32[128,2,128]{2,1,0:T(2,128)} copy(f32[128,2,128]{2,0,1:T(8,128)} %bitcast.3) | data formatting | bytes 262144
  46.1 1.6 %copy.9 = f32[16,16,128]{2,1,0:T(8,128)} copy(f32[16,16,128]{2,1,0:T(8,128)} %get-tuple-element.10) | data formatting | bytes 262144

commit v3 on v2

--- a/solution.py
+++ b/solution.py
@@ -33,23 +33,22 @@
     term_hbm,
     part_hbm,
     share_hbm,
-    costate_hbm,
-    clear_hbm,
+    costate,
+    clear,
     maps,
     force,
     term,
     part,
     share,
     offsets,
+    unit,
     outgoing,
     incoming,
     edges,
     starts,
-    costate,
     flow,
     traded,
     mixer,
-    clear,
     load_sem,
     small_sem,
     map_send,
@@ -58,7 +57,6 @@
     edge_recv,
     flow_send,
     flow_recv,
-    out_sem,
 ):
     rows, per, sec = force.shape
     here, zone = lax.axis_index("period"), lax.axis_index("region")
@@ -91,10 +89,9 @@
         )
     ]
     small[0].start()
-    for k in range(batches):
-        for c in range(4):
-            for i in range(BATCH):
-                load(k, c, i).start()
+    for c in range(4):
+        for i in range(BATCH):
+            load(0, c, i).start()
     for copy in small[1:]:
         copy.start()
 
@@ -110,6 +107,7 @@
 
     square = (sec, sec)
     eye = lax.broadcasted_iota(jnp.int32, square, 0) == lax.broadcasted_iota(jnp.int32, square, 1)
+    unit[...] = jnp.where(eye, 1.0, 0.0)
     top = lax.broadcasted_iota(jnp.int32, (16, sec), 0) == 0
 
     def send_map(k, i):
@@ -129,6 +127,12 @@
     small[0].wait()
 
     def compose(k, carry):
+        @pl.when(k < batches - 1)
+        def _():
+            for c in range(4):
+                for i in range(BATCH):
+                    load(k + 1, c, i).start()
+
         for c in range(4):
             for i in range(BATCH):
                 load(k, c, i).wait()
@@ -142,8 +146,7 @@
                         prod = block.T
                         offset = jnp.broadcast_to(source, (8, sec))
                     else:
-                        diag = jnp.sum(jnp.where(eye, block, 0.0), axis=0, keepdims=True)
-                        high, low = split(jnp.where(eye, 0.0, block))
+                        high, low = split(block - unit[...])
                         late, late_offset = maps[slot, t + 1], offsets[slot, t + 1 : t + 2]
                         late_high, late_low = split(late)
                         tail_high, tail_low = split(jnp.where(top, late_offset, 0.0))
@@ -154,8 +157,8 @@
                             jnp.concatenate([high, high, low], 1),
                             NT,
                         )
-                        offset = prod[sec : sec + 8] + late_offset * diag + source
-                        prod = prod[:sec] + late * diag
+                        offset = prod[sec : sec + 8] + late_offset + source
+                        prod = prod[:sec] + late
                     maps[slot, t] = prod
                     offsets[slot, t : t + 1] = offset[:1]
                     if t == 0:
@@ -314,8 +317,6 @@
         for step in range(1, nreg):
             send_flow(lax.rem(zone + step, nreg), h).start()
         keep_flow(h).start()
-    save = pltpu.make_async_copy(costate, costate_hbm, out_sem.at[0])
-    save.start()
 
     for part_no in range(2):
         h = lax.rem(lax.div(here, half) + part_no, 2)
@@ -340,8 +341,6 @@
     result = whole - mixed
     for t in range(share_t):
         clear[t] = result[:, t * sec : (t + 1) * sec]
-    done = pltpu.make_async_copy(clear, clear_hbm, out_sem.at[1])
-    done.start()
 
     def drain(row, carry):
         @pl.when(row != here)
@@ -359,8 +358,6 @@
     for step in range(1, nreg):
         for h in range(2):
             send_flow(lax.rem(zone + step, nreg), h).wait_send()
-    save.wait()
-    done.wait()
 
 
 def shards(nper, nreg, transition, forcing, terminal, partners, shares):
@@ -373,11 +370,11 @@
     costate, clearing = pl.pallas_call(
         functools.partial(kernel, nper, nreg),
         out_shape=(
-            jax.ShapeDtypeStruct((rows, per, sec), F32),
-            jax.ShapeDtypeStruct((share_t, regions, sec), F32),
+            pltpu.VMEM((rows, per, sec), F32),
+            pltpu.VMEM((share_t, regions, sec), F32),
         ),
         in_specs=[anywhere] * 5,
-        out_specs=[anywhere] * 2,
+        out_specs=[pl.BlockSpec(memory_space=pltpu.VMEM)] * 2,
         scratch_shapes=[
             pltpu.VMEM((rows, per, sec, sec), F32),
             pltpu.VMEM((rows, per, sec), F32),
@@ -385,15 +382,14 @@
             pltpu.VMEM(ids.shape, jnp.int32),
             pltpu.VMEM(amounts.shape, F32),
             pltpu.VMEM((rows, per, sec), F32),
+            pltpu.VMEM((sec, sec), F32),
             pltpu.VMEM((rows, sec + 8, sec), F32),
             pltpu.VMEM((nper, sec + 8, sec), F32),
             pltpu.VMEM((nper, 1, sec), F32),
             pltpu.VMEM((rows, 1, sec), F32),
-            pltpu.VMEM((rows, per, sec), F32),
             pltpu.VMEM((per, rows, sec), F32),
             pltpu.VMEM((share_t, regions, sec), F32),
             pltpu.VMEM((BLOCKS // 2, 2 * regions, 2 * regions), BF16),
-            pltpu.VMEM((share_t, regions, sec), F32),
             dma((rows // BATCH, 4, BATCH)),
             dma((4,)),
             dma((rows,)),
@@ -402,7 +398,6 @@
             dma((rows,)),
             dma((nreg, 2)),
             dma((nreg, 2)),
-            dma((2,)),
         ],
         compiler_params=pltpu.CompilerParams(
             collective_id=0, has_side_effects=True, vmem_limit_bytes=60 * 2**20

time: 47.8 us -> 41.8 us (0.87)
  Pallas kernels: 43.8 us -> 39.6 us
  local copies, waits for them, and re-layouts: 3.23 us -> 1.41 us
    pallas_call x1, Pallas kernels: 43.8 us -> 39.6 us  [shards(): pl.pallas_call(functools.partial(kernel, nper, nreg), out_shape=(pltpu.VM...]
    unnamed x2, local copies, waits for them, and re-layouts: 3.23 us -> 1.41 us
where the time goes in v3:
time: 41.8 us; the launch traced here: 41.7 us
  Pallas kernels  39.6 us (95%)
  local copies, waits for them, and re-layouts  1.41 us (3%)
  between operations  0.64 us (2%)
    pallas_call x1, Pallas kernels, shards(): pl.pallas_call(functools.partial(kernel, nper, nreg), out_shape=(pltpu.VM...  39.6 us
    unnamed x2, local copies, waits for them, and re-layouts  1.41 us

profile of v3, /device:TPU:1, one launch (start us, length us, event | category | flops | bytes accessed | tf_op | source)
XLA Modules:
  0.0 41.7 jit_solution(14743972982277720676)
XLA Ops:
  0.6 39.6 %newton_step.1 = (f32[16,16,128]{2,1,0:T(8,128)S(1)}, f32[2,128,128]{2,1,0:T(8,128)S(1)}) custom-call(f32[16,16,128,128]{3,2,1,0:T(8,128)} %trans_hbm.1, f32[16,16,128]{2,1,0:T(8,128)} %force_hbm.1, f32[16,128]{1,0:T(8,128)} %term_hbm.1, s32[8,8,128]{2,1,0:T(8,128)} %bitcast.4, f32[8,8,128]{2,1,0:T(8,128)} %bitcast.5), custom_call_target="tpu_custom_call" | custom-call | tf_op jit(solution)/shard_map/newton_step/pallas_call | solution.py:370
  40.3 0.7 %copy.9 = f32[16,16,128]{2,1,0:T(8,128)} copy(f32[16,16,128]{2,1,0:T(8,128)S(1)} %get-tuple-element.8) | data formatting | bytes 262144
  40.9 0.8 %copy.7 = f32[128,2,128]{2,1,0:T(2,128)} copy(f32[128,2,128]{2,0,1:T(8,128)S(1)} %bitcast.3) | data formatting | bytes 262144

commit v4 on v3

--- a/solution.py
+++ b/solution.py
@@ -34,7 +34,8 @@
     part_hbm,
     share_hbm,
     costate,
-    clear,
+    traded,
+    mixer,
     maps,
     force,
     term,
@@ -44,15 +45,17 @@
     unit,
     outgoing,
     incoming,
+    shifts,
+    given,
     edges,
     starts,
     flow,
-    traded,
-    mixer,
     load_sem,
     small_sem,
     map_send,
     map_recv,
+    shift_send,
+    shift_recv,
     edge_send,
     edge_recv,
     flow_send,
@@ -65,6 +68,16 @@
     share_t = per // nreg
     half = rows // 2
 
+    barrier = pltpu.get_barrier_semaphore()
+    for step in range(1, nper):
+        pl.semaphore_signal(
+            barrier, inc=1, device_id=(lax.rem(here + step, nper), zone), device_id_type=MESH
+        )
+    for step in range(1, nreg):
+        pl.semaphore_signal(
+            barrier, inc=1, device_id=(here, lax.rem(zone + step, nreg)), device_id_type=MESH
+        )
+
     def row_of(k, i):
         skew = k + lax.div(k, 2) * (1 - 2 * lax.rem(k, 2))
         along_x = lax.rem(lax.div(here, BATCH) + i, batches)
@@ -95,34 +108,35 @@
     for copy in small[1:]:
         copy.start()
 
-    barrier = pltpu.get_barrier_semaphore()
-    for step in range(1, nper):
-        pl.semaphore_signal(
-            barrier, inc=1, device_id=(lax.rem(here + step, nper), zone), device_id_type=MESH
-        )
-    for step in range(1, nreg):
-        pl.semaphore_signal(
-            barrier, inc=1, device_id=(here, lax.rem(zone + step, nreg)), device_id_type=MESH
-        )
-
     square = (sec, sec)
     eye = lax.broadcasted_iota(jnp.int32, square, 0) == lax.broadcasted_iota(jnp.int32, square, 1)
     unit[...] = jnp.where(eye, 1.0, 0.0)
     top = lax.broadcasted_iota(jnp.int32, (16, sec), 0) == 0
 
+    def move_map(slot, source, target):
+        return [
+            pltpu.make_async_remote_copy(
+                src_ref=src.at[slot],
+                dst_ref=dst.at[source],
+                send_sem=send.at[slot],
+                recv_sem=recv.at[source],
+                device_id=(target, zone),
+                device_id_type=MESH,
+            )
+            for src, dst, send, recv in [
+                (outgoing, incoming, map_send, map_recv),
+                (shifts, given, shift_send, shift_recv),
+            ]
+        ]
+
     def send_map(k, i):
-        row, slot = row_of(k, i), k * BATCH + i
-        return pltpu.make_async_remote_copy(
-            src_ref=outgoing.at[slot],
-            dst_ref=incoming.at[here],
-            send_sem=map_send.at[slot],
-            recv_sem=map_recv.at[here],
-            device_id=(row, zone),
-            device_id_type=MESH,
-        )
+        return move_map(k * BATCH + i, here, row_of(k, i))
 
     def keep_map():
-        return pltpu.make_async_copy(outgoing.at[0], incoming.at[here], map_recv.at[here])
+        return [
+            pltpu.make_async_copy(outgoing.at[0], incoming.at[here], map_recv.at[here]),
+            pltpu.make_async_copy(shifts.at[0], given.at[here], shift_recv.at[here]),
+        ]
 
     small[0].wait()
 
@@ -162,8 +176,8 @@
                     maps[slot, t] = prod
                     offsets[slot, t : t + 1] = offset[:1]
                     if t == 0:
-                        outgoing[slot, :sec] = prod
-                        outgoing[slot, sec:] = offset
+                        outgoing[slot] = prod
+                        shifts[slot] = offset[:1]
 
         @pl.when(k == 0)
         def _():
@@ -174,11 +188,13 @@
 
             @pl.when((row != here) & (here != 0))
             def _(i=i):
-                send_map(k, i).start()
+                for copy in send_map(k, i):
+                    copy.start()
 
             @pl.when((row == here) & (here != 0))
             def _():
-                keep_map().start()
+                for copy in keep_map():
+                    copy.start()
 
         return carry
 
@@ -231,22 +247,17 @@
 
         @pl.when(p != here)
         def _():
-            pltpu.make_async_remote_copy(
-                src_ref=outgoing.at[p],
-                dst_ref=incoming.at[p],
-                send_sem=map_send.at[p],
-                recv_sem=map_recv.at[p],
-                device_id=(p, zone),
-                device_id_type=MESH,
-            ).wait_recv()
+            for copy in move_map(p, p, p):
+                copy.wait_recv()
 
         @pl.when(p == here)
         def _():
-            keep_map().wait()
+            for copy in keep_map():
+                copy.wait()
 
         ship_edge(p)
-        moved = incoming[p, :sec] * upright(state)
-        state = jnp.sum(moved, axis=0, keepdims=True) + incoming[p, sec : sec + 1]
+        moved = incoming[p] * upright(state)
+        state = jnp.sum(moved, axis=0, keepdims=True) + given[p]
         edges[p - 1] = state
         return state
 
@@ -318,12 +329,35 @@
             send_flow(lax.rem(zone + step, nreg), h).start()
         keep_flow(h).start()
 
+    def drain(row, carry):
+        @pl.when(row != here)
+        def _():
+            send_edge(row).wait_send()
+
+        @pl.when((row > 0) & (here != 0))
+        def _():
+            for copy in move_map(row, here, row):
+                copy.wait_send()
+
+        return carry
+
+    lax.fori_loop(0, rows, drain, 0)
+
     for part_no in range(2):
         h = lax.rem(lax.div(here, half) + part_no, 2)
         for step in range(1, nreg):
             got_flow(lax.rem(zone + step, nreg), h).wait_recv()
         keep_flow(h).wait()
 
+    for step in range(1, nreg):
+        for h in range(2):
+            send_flow(lax.rem(zone + step, nreg), h).wait_send()
+
+
+def mix(traded, mixer, costate, costate_hbm, clear_hbm, clear, out_sem):
+    share_t, sec = traded.shape[0], traded.shape[2]
+    save = pltpu.make_async_copy(costate, costate_hbm, out_sem.at[0])
+    save.start()
     width = share_t * sec
     whole = jnp.concatenate([traded[t] for t in range(share_t)], 1)
     high, low = split(whole)
@@ -340,24 +374,11 @@
         mixed += dot(mixer[pair, :sec], tall_low, NN)
     result = whole - mixed
     for t in range(share_t):
-        clear[t] = result[:, t * sec : (t + 1) * sec]
-
-    def drain(row, carry):
-        @pl.when(row != here)
-        def _():
-            send_edge(row).wait_send()
-
-        @pl.when((row > 0) & (here != 0))
-        def _():
-            send_map(lax.div(row, BATCH), lax.rem(row, BATCH)).wait_send()
-
-        return carry
-
-    lax.fori_loop(0, rows, drain, 0)
-
-    for step in range(1, nreg):
-        for h in range(2):
-            send_flow(lax.rem(zone + step, nreg), h).wait_send()
+        clear[:, t, :] = result[:, t * sec : (t + 1) * sec]
+    done = pltpu.make_async_copy(clear, clear_hbm, out_sem.at[1])
+    done.start()
+    save.wait()
+    done.wait()
 
 
 def shards(nper, nreg, transition, forcing, terminal, partners, shares):
@@ -366,15 +387,17 @@
     share_t = per // nreg
     ids, amounts = jnp.swapaxes(partners, 1, 2), jnp.swapaxes(shares, 1, 2)
     anywhere = pl.BlockSpec(memory_space=pl.ANY)
+    local = pl.BlockSpec(memory_space=pltpu.VMEM)
     dma = pltpu.SemaphoreType.DMA
-    costate, clearing = pl.pallas_call(
+    costate, traded, mixer = pl.pallas_call(
         functools.partial(kernel, nper, nreg),
         out_shape=(
             pltpu.VMEM((rows, per, sec), F32),
             pltpu.VMEM((share_t, regions, sec), F32),
+            pltpu.VMEM((BLOCKS // 2, 2 * regions, 2 * regions), BF16),
         ),
         in_specs=[anywhere] * 5,
-        out_specs=[pl.BlockSpec(memory_space=pltpu.VMEM)] * 2,
+        out_specs=[local] * 3,
         scratch_shapes=[
             pltpu.VMEM((rows, per, sec, sec), F32),
             pltpu.VMEM((rows, per, sec), F32),
@@ -383,15 +406,17 @@
             pltpu.VMEM(amounts.shape, F32),
             pltpu.VMEM((rows, per, sec), F32),
             pltpu.VMEM((sec, sec), F32),
-            pltpu.VMEM((rows, sec + 8, sec), F32),
-            pltpu.VMEM((nper, sec + 8, sec), F32),
+            pltpu.VMEM((rows, sec, sec), F32),
+            pltpu.VMEM((nper, sec, sec), F32),
+            pltpu.VMEM((rows, 1, sec), F32),
+            pltpu.VMEM((nper, 1, sec), F32),
             pltpu.VMEM((nper, 1, sec), F32),
             pltpu.VMEM((rows, 1, sec), F32),
             pltpu.VMEM((per, rows, sec), F32),
-            pltpu.VMEM((share_t, regions, sec), F32),
-            pltpu.VMEM((BLOCKS // 2, 2 * regions, 2 * regions), BF16),
             dma((rows // BATCH, 4, BATCH)),
             dma((4,)),
+            dma((rows,)),
+            dma((nper,)),
             dma((rows,)),
             dma((nper,)),
             dma((nper,)),
@@ -404,7 +429,18 @@
         ),
         name="newton_step",
     )(transition, forcing, terminal, ids, amounts)
-    return costate, jnp.swapaxes(clearing, 0, 1)
+    return pl.pallas_call(
+        mix,
+        out_shape=(
+            jax.ShapeDtypeStruct((rows, per, sec), F32),
+            jax.ShapeDtypeStruct((regions, share_t, sec), F32),
+        ),
+        in_specs=[local] * 3,
+        out_specs=[anywhere] * 2,
+        scratch_shapes=[pltpu.VMEM((regions, share_t, sec), F32), dma((2,))],
+        compiler_params=pltpu.CompilerParams(vmem_limit_bytes=8 * 2**20),
+        name="trade_mix",
+    )(traded, mixer, costate)
 
 
 def solution(mesh):

time: 41.8 us -> 41.5 us (level)
  local copies, waits for them, and re-layouts: 1.41 us -> 0 us
  Pallas kernels: 39.6 us -> 40.8 us
    unnamed x2 -> x0, local copies, waits for them, and re-layouts: 1.41 us -> none
    pallas_call x0 -> x1, Pallas kernels: none -> 1.12 us  [shards(): pl.pallas_call(mix, out_shape=(jax.ShapeDtypeStruct((rows, per, sec), F32...]
where the time goes in v4:
time: 41.5 us; the launch traced here: 41.4 us
  Pallas kernels  40.8 us (98%)
  between operations  0.64 us (2%)
    pallas_call x1, Pallas kernels, shards(): pl.pallas_call(functools.partial(kernel, nper, nreg), out_shape=(pltpu.VM...  39.6 us
    pallas_call x1, Pallas kernels, shards(): pl.pallas_call(mix, out_shape=(jax.ShapeDtypeStruct((rows, per, sec), F32...  1.12 us

profile of v4, /device:TPU:1, one launch (start us, length us, event | category | flops | bytes accessed | tf_op | source)
XLA Modules:
  0.0 41.4 jit_solution(17512016051049056840)
XLA Ops:
  0.6 39.6 %newton_step.1 = (f32[16,16,128]{2,1,0:T(8,128)S(1)}, f32[2,128,128]{2,1,0:T(8,128)S(1)}, bf16[4,256,256]{2,1,0:T(8,128)(2,1)S(1)}) custom-call(f32[16,16,128,128]{3,2,1,0:T(8,128)} %trans_hbm.1, f32[16,16,128]{2,1,0:T(8,128)} %force_hbm.1, f32[16,128]{1,0:T(8,128)} %term_hbm.1, s32[8,8,128]{2,1,0:T(8,128)} %bitcast.2, f32[8,8,128]{2,1,0:T(8,128)} %bitcast.3), custom_call_target="tpu_custom_call" | custom-call | tf_op jit(solution)/shard_map/newton_step/pallas_call | solution.py:392
  40.3 1.1 %trade_mix.1 = (f32[16,16,128]{2,1,0:T(8,128)}, f32[128,2,128]{2,1,0:T(2,128)}) custom-call(f32[2,128,128]{2,1,0:T(8,128)S(1)} %get-tuple-element.5.traded, bf16[4,256,256]{2,1,0:T(8,128)(2,1)S(1)} %get-tuple-element.6.mixer, f32[16,16,128]{2,1,0:T(8,128)S(1)} %get-tuple-element.7.costate), custom_call_target="tpu_custom_call" | custom-call | tf_op jit(solution)/shard_map/trade_mix/pallas_call | solution.py:432

commit v5 on v4

--- a/solution.py
+++ b/solution.py
@@ -49,6 +49,7 @@
     given,
     edges,
     starts,
+    columns,
     flow,
     load_sem,
     small_sem,
@@ -66,7 +67,6 @@
     batches = rows // BATCH
     chunk = per // 4
     share_t = per // nreg
-    half = rows // 2
 
     barrier = pltpu.get_barrier_semaphore()
     for step in range(1, nper):
@@ -82,12 +82,6 @@
         skew = k + lax.div(k, 2) * (1 - 2 * lax.rem(k, 2))
         along_x = lax.rem(lax.div(here, BATCH) + i, batches)
         return along_x * BATCH + lax.rem(here + i + skew, BATCH)
-
-    def slot_of(row):
-        i = lax.rem(lax.div(row, BATCH) + batches - lax.div(here, BATCH), batches)
-        skew = lax.rem(row + 2 * BATCH - lax.rem(here, BATCH) - i, BATCH)
-        k = skew + lax.div(skew, 2) * (1 - 2 * lax.rem(skew, 2))
-        return k * BATCH + i
 
     def load(k, c, i):
         when = pl.ds(per - chunk * (c + 1), chunk)
@@ -264,70 +258,79 @@
     lax.fori_loop(0, nper - 1, chain, state)
     ship_edge(0)
 
-    def finish(i, carry):
-        row = lax.rem(lax.div(here, half) * half + i, rows)
-        slot = slot_of(row)
-
-        @pl.when(row != here)
-        def _():
-            pltpu.make_async_remote_copy(
-                src_ref=edges.at[row],
-                dst_ref=starts.at[row],
-                send_sem=edge_send.at[row],
-                recv_sem=edge_recv.at[row],
-                device_id=(row, zone),
-                device_id_type=MESH,
-            ).wait_recv()
-
-        @pl.when(row == here)
-        def _():
-            keep_edge().wait()
-
-        column = jnp.broadcast_to(upright(starts[row]), square)
-        lines = [jnp.sum(maps[slot, t] * column, axis=0, keepdims=True) for t in range(per)]
-        value = jnp.concatenate(lines, 0) + offsets[slot]
-        costate[row] = value
-        bent = jnp.tanh(value)
-        for t in range(per):
-            flow[t, pl.ds(row, 1), :] = bent[t : t + 1]
+    def arrive(k, carry):
+        for i in range(BATCH):
+            row = row_of(k, i)
+
+            @pl.when(row != here)
+            def _(row=row):
+                pltpu.make_async_remote_copy(
+                    src_ref=edges.at[row],
+                    dst_ref=starts.at[row],
+                    send_sem=edge_send.at[row],
+                    recv_sem=edge_recv.at[row],
+                    device_id=(row, zone),
+                    device_id_type=MESH,
+                ).wait_recv()
+
+            @pl.when(row == here)
+            def _():
+                keep_edge().wait()
+
+        for i in range(BATCH):
+            column = upright(starts[row_of(k, i)])
+            columns[k * BATCH + i] = jnp.broadcast_to(column, square)
         return carry
 
-    def send_flow(other, h):
-        mine = pl.multiple_of(zone * rows + h * half, 8)
+    lax.fori_loop(0, batches, arrive, 0)
+
+    def send_flow(other):
         return pltpu.make_async_remote_copy(
-            src_ref=flow.at[pl.ds(other * share_t, share_t), pl.ds(h * half, half)],
-            dst_ref=traded.at[:, pl.ds(mine, half)],
-            send_sem=flow_send.at[other, h],
-            recv_sem=flow_recv.at[zone, h],
+            src_ref=flow.at[pl.ds(other * share_t, share_t)],
+            dst_ref=traded.at[:, pl.ds(pl.multiple_of(zone * rows, 8), rows)],
+            send_sem=flow_send.at[other],
+            recv_sem=flow_recv.at[zone],
             device_id=(here, other),
             device_id_type=MESH,
         )
 
-    def keep_flow(h):
-        mine = pl.multiple_of(zone * rows + h * half, 8)
+    def keep_flow():
         return pltpu.make_async_copy(
-            flow.at[pl.ds(zone * share_t, share_t), pl.ds(h * half, half)],
-            traded.at[:, pl.ds(mine, half)],
-            flow_recv.at[zone, h],
-        )
-
-    def got_flow(other, h):
-        theirs = pl.multiple_of(other * rows + h * half, 8)
+            flow.at[pl.ds(zone * share_t, share_t)],
+            traded.at[:, pl.ds(pl.multiple_of(zone * rows, 8), rows)],
+            flow_recv.at[zone],
+        )
+
+    def got_flow(other):
         return pltpu.make_async_remote_copy(
-            src_ref=flow.at[pl.ds(other * share_t, share_t), pl.ds(h * half, half)],
-            dst_ref=traded.at[:, pl.ds(theirs, half)],
-            send_sem=flow_send.at[other, h],
-            recv_sem=flow_recv.at[other, h],
+            src_ref=flow.at[pl.ds(other * share_t, share_t)],
+            dst_ref=traded.at[:, pl.ds(pl.multiple_of(other * rows, 8), rows)],
+            send_sem=flow_send.at[other],
+            recv_sem=flow_recv.at[other],
             device_id=(here, other),
             device_id_type=MESH,
         )
 
-    for part_no in range(2):
-        lax.fori_loop(part_no * half, (part_no + 1) * half, finish, 0)
-        h = lax.rem(lax.div(here, half) + part_no, 2)
-        for step in range(1, nreg):
-            send_flow(lax.rem(zone + step, nreg), h).start()
-        keep_flow(h).start()
+    layers = nreg // 2
+    order = [(dz, dc) for dz in (2, 1, 3, 0) if dz < layers for dc in (1, 0)]
+    others = []
+    for dz, dc in order:
+        other = lax.rem(lax.div(zone, 2) + dz, layers) * 2 + lax.rem(zone + dc, 2)
+        for step in range(share_t):
+            t = other * share_t + step
+            for k in range(batches):
+                for i in range(BATCH):
+                    slot, row = k * BATCH + i, row_of(k, i)
+                    value = jnp.sum(maps[slot, t] * columns[slot], axis=0, keepdims=True)
+                    value += offsets[slot, pl.ds(t, 1), :]
+                    costate[row, pl.ds(t, 1), :] = value
+                    flow[t, pl.ds(row, 1), :] = value
+            flow[t] = jnp.tanh(flow[t])
+        if (dz, dc) != (0, 0):
+            others.append(other)
+            send_flow(other).start()
+        else:
+            keep_flow().start()
 
     def drain(row, carry):
         @pl.when(row != here)
@@ -343,15 +346,11 @@
 
     lax.fori_loop(0, rows, drain, 0)
 
-    for part_no in range(2):
-        h = lax.rem(lax.div(here, half) + part_no, 2)
-        for step in range(1, nreg):
-            got_flow(lax.rem(zone + step, nreg), h).wait_recv()
-        keep_flow(h).wait()
-
-    for step in range(1, nreg):
-        for h in range(2):
-            send_flow(lax.rem(zone + step, nreg), h).wait_send()
+    keep_flow().wait()
+    for other in others:
+        got_flow(other).wait_recv()
+    for other in others:
+        send_flow(other).wait_send()
 
 
 def mix(traded, mixer, costate, costate_hbm, clear_hbm, clear, out_sem):
@@ -412,6 +411,7 @@
             pltpu.VMEM((nper, 1, sec), F32),
             pltpu.VMEM((nper, 1, sec), F32),
             pltpu.VMEM((rows, 1, sec), F32),
+            pltpu.VMEM((rows, sec, sec), F32),
             pltpu.VMEM((per, rows, sec), F32),
             dma((rows // BATCH, 4, BATCH)),
             dma((4,)),
@@ -421,8 +421,8 @@
             dma((nper,)),
             dma((nper,)),
             dma((rows,)),
-            dma((nreg, 2)),
-            dma((nreg, 2)),
+            dma((nreg,)),
+            dma((nreg,)),
         ],
         compiler_params=pltpu.CompilerParams(
             collective_id=0, has_side_effects=True, vmem_limit_bytes=60 * 2**20

time: 41.5 us -> 39.7 us (0.957)
  Pallas kernels: 40.8 us -> 39 us
    pallas_call x1, Pallas kernels: 39.6 us -> 37.9 us  [shards(): pl.pallas_call(functools.partial(kernel, nper, nreg), out_shape=(pltpu.VM...]
where the time goes in v5:
time: 39.7 us; the launch traced here: 39.6 us
  Pallas kernels  39 us (98%)
  between operations  0.64 us (2%)
    pallas_call x1, Pallas kernels, shards(): pl.pallas_call(functools.partial(kernel, nper, nreg), out_shape=(pltpu.VM...  37.9 us
    pallas_call x1, Pallas kernels, shards(): pl.pallas_call(mix, out_shape=(jax.ShapeDtypeStruct((rows, per, sec), F32...  1.12 us

profile of v5, /device:TPU:1, one launch (start us, length us, event | category | flops | bytes accessed | tf_op | source)
XLA Modules:
  0.0 39.6 jit_solution(3522227403223246343)
XLA Ops:
  0.6 37.9 %newton_step.1 = (f32[16,16,128]{2,1,0:T(8,128)S(1)}, f32[2,128,128]{2,1,0:T(8,128)S(1)}, bf16[4,256,256]{2,1,0:T(8,128)(2,1)S(1)}) custom-call(f32[16,16,128,128]{3,2,1,0:T(8,128)} %trans_hbm.1, f32[16,16,128]{2,1,0:T(8,128)} %force_hbm.1, f32[16,128]{1,0:T(8,128)} %term_hbm.1, s32[8,8,128]{2,1,0:T(8,128)} %bitcast.2, f32[8,8,128]{2,1,0:T(8,128)} %bitcast.3), custom_call_target="tpu_custom_call" | custom-call | tf_op jit(solution)/shard_map/newton_step/pallas_call | solution.py:391
  38.5 1.1 %trade_mix.1 = (f32[16,16,128]{2,1,0:T(8,128)}, f32[128,2,128]{2,1,0:T(2,128)}) custom-call(f32[2,128,128]{2,1,0:T(8,128)S(1)} %get-tuple-element.5.traded, bf16[4,256,256]{2,1,0:T(8,128)(2,1)S(1)} %get-tuple-element.6.mixer, f32[16,16,128]{2,1,0:T(8,128)S(1)} %get-tuple-element.7.costate), custom_call_target="tpu_custom_call" | custom-call | tf_op jit(solution)/shard_map/trade_mix/pallas_call | solution.py:432

commit v6 on v5

--- a/solution.py
+++ b/solution.py
@@ -78,10 +78,15 @@
             barrier, inc=1, device_id=(here, lax.rem(zone + step, nreg)), device_id_type=MESH
         )
 
+    swapped = lax.rem(zone, 2) == 1
+    at_x, at_y = lax.div(here, BATCH), lax.rem(here, BATCH)
+    last = nper - 1
+
     def row_of(k, i):
         skew = k + lax.div(k, 2) * (1 - 2 * lax.rem(k, 2))
-        along_x = lax.rem(lax.div(here, BATCH) + i, batches)
-        return along_x * BATCH + lax.rem(here + i + skew, BATCH)
+        other = lax.rem(i + skew, BATCH)
+        along_x, along_y = jnp.where(swapped, other, i), jnp.where(swapped, i, other)
+        return lax.rem(at_x + along_x, batches) * BATCH + lax.rem(at_y + along_y, BATCH)
 
     def load(k, c, i):
         when = pl.ds(per - chunk * (c + 1), chunk)
@@ -95,17 +100,19 @@
             [(force_hbm, force), (term_hbm, term), (part_hbm, part), (share_hbm, share)]
         )
     ]
-    small[0].start()
+    for copy in small:
+        copy.start()
     for c in range(4):
         for i in range(BATCH):
             load(0, c, i).start()
-    for copy in small[1:]:
-        copy.start()
 
     square = (sec, sec)
     eye = lax.broadcasted_iota(jnp.int32, square, 0) == lax.broadcasted_iota(jnp.int32, square, 1)
     unit[...] = jnp.where(eye, 1.0, 0.0)
     top = lax.broadcasted_iota(jnp.int32, (16, sec), 0) == 0
+
+    def upright(vector):
+        return jnp.sum(jnp.where(eye, vector, 0.0), axis=1, keepdims=True)
 
     def move_map(slot, source, target):
         return [
@@ -132,7 +139,8 @@
             pltpu.make_async_copy(shifts.at[0], given.at[here], shift_recv.at[here]),
         ]
 
-    small[0].wait()
+    for copy in small[:2]:
+        copy.wait()
 
     def compose(k, carry):
         @pl.when(k < batches - 1)
@@ -177,24 +185,38 @@
         def _():
             pl.semaphore_wait(barrier, nper + nreg - 2)
 
+        @pl.when(here == last)
+        def _():
+            for i in range(BATCH):
+                slot = k * BATCH + i
+                column = upright(term[pl.ds(row_of(k, i), 1), :])
+                value = jnp.sum(maps[slot, 0] * column, axis=0, keepdims=True)
+                shifts[slot] = value + offsets[slot, 0:1]
+
         for i in (2, 1, 3, 0):
             row = row_of(k, i)
 
             @pl.when((row != here) & (here != 0))
             def _(i=i):
-                for copy in send_map(k, i):
-                    copy.start()
+                send_map(k, i)[1].start()
+
+            @pl.when((row != here) & (here != 0) & (here != last))
+            def _(i=i):
+                send_map(k, i)[0].start()
 
             @pl.when((row == here) & (here != 0))
             def _():
-                for copy in keep_map():
-                    copy.start()
+                keep_map()[1].start()
+
+            @pl.when((row == here) & (here != 0) & (here != last))
+            def _():
+                keep_map()[0].start()
 
         return carry
 
     lax.fori_loop(0, batches, compose, 0)
 
-    for copy in small[1:]:
+    for copy in small[2:]:
         copy.wait()
 
     region = lax.broadcasted_iota(jnp.int32, square, 0)
@@ -208,9 +230,6 @@
         mixer[g // 2, :sec, side : side + sec] = high
         mixer[g // 2, sec:, side : side + sec] = low
 
-    def upright(vector):
-        return jnp.sum(jnp.where(eye, vector, 0.0), axis=1, keepdims=True)
-
     def send_edge(p):
         return pltpu.make_async_remote_copy(
             src_ref=edges.at[p],
@@ -233,11 +252,22 @@
         def _():
             keep_edge().start()
 
-    state = term[pl.ds(here, 1), :]
-    edges[nper - 1] = state
+    edges[last] = term[pl.ds(here, 1), :]
+    ship_edge(last)
+
+    @pl.when(here != last)
+    def _():
+        move_map(last, last, last)[1].wait_recv()
+
+    @pl.when(here == last)
+    def _():
+        keep_map()[1].wait()
+
+    state = given[last]
+    edges[last - 1] = state
 
     def chain(step, state):
-        p = nper - 1 - step
+        p = last - 1 - step
 
         @pl.when(p != here)
         def _():
@@ -255,34 +285,32 @@
         edges[p - 1] = state
         return state
 
-    lax.fori_loop(0, nper - 1, chain, state)
+    lax.fori_loop(0, nper - 2, chain, state)
     ship_edge(0)
 
-    def arrive(k, carry):
-        for i in range(BATCH):
-            row = row_of(k, i)
-
-            @pl.when(row != here)
-            def _(row=row):
-                pltpu.make_async_remote_copy(
-                    src_ref=edges.at[row],
-                    dst_ref=starts.at[row],
-                    send_sem=edge_send.at[row],
-                    recv_sem=edge_recv.at[row],
-                    device_id=(row, zone),
-                    device_id_type=MESH,
-                ).wait_recv()
-
-            @pl.when(row == here)
-            def _():
-                keep_edge().wait()
-
+    def arrive(row, carry):
+        @pl.when(row != here)
+        def _():
+            pltpu.make_async_remote_copy(
+                src_ref=edges.at[row],
+                dst_ref=starts.at[row],
+                send_sem=edge_send.at[row],
+                recv_sem=edge_recv.at[row],
+                device_id=(row, zone),
+                device_id_type=MESH,
+            ).wait_recv()
+
+        @pl.when(row == here)
+        def _():
+            keep_edge().wait()
+
+        return carry
+
+    lax.fori_loop(0, rows, arrive, 0)
+    for k in range(batches):
         for i in range(BATCH):
             column = upright(starts[row_of(k, i)])
             columns[k * BATCH + i] = jnp.broadcast_to(column, square)
-        return carry
-
-    lax.fori_loop(0, batches, arrive, 0)
 
     def send_flow(other):
         return pltpu.make_async_remote_copy(
@@ -339,8 +367,11 @@
 
         @pl.when((row > 0) & (here != 0))
         def _():
-            for copy in move_map(row, here, row):
-                copy.wait_send()
+            move_map(row, here, row)[1].wait_send()
+
+        @pl.when((row > 0) & (here != 0) & (here != last))
+        def _():
+            move_map(row, here, row)[0].wait_send()
 
         return carry
 

time: 39.7 us -> 39.7 us (level)
  no operation moved by 1% of the time
where the time goes in v6:
time: 39.7 us; the launch traced here: 39.6 us
  Pallas kernels  38.9 us (98%)
  between operations  0.64 us (2%)
    pallas_call x1, Pallas kernels, shards(): pl.pallas_call(functools.partial(kernel, nper, nreg), out_shape=(pltpu.VM...  37.8 us
    pallas_call x1, Pallas kernels, shards(): pl.pallas_call(mix, out_shape=(jax.ShapeDtypeStruct((rows, per, sec), F32...  1.12 us

profile of v6, /device:TPU:1, one launch (start us, length us, event | category | flops | bytes accessed | tf_op | source)
XLA Modules:
  0.0 39.6 jit_solution(404940084661408350)
XLA Ops:
  0.6 37.8 %newton_step.1 = (f32[16,16,128]{2,1,0:T(8,128)S(1)}, f32[2,128,128]{2,1,0:T(8,128)S(1)}, bf16[4,256,256]{2,1,0:T(8,128)(2,1)S(1)}) custom-call(f32[16,16,128,128]{3,2,1,0:T(8,128)} %trans_hbm.1, f32[16,16,128]{2,1,0:T(8,128)} %force_hbm.1, f32[16,128]{1,0:T(8,128)} %term_hbm.1, s32[8,8,128]{2,1,0:T(8,128)} %bitcast.2, f32[8,8,128]{2,1,0:T(8,128)} %bitcast.3), custom_call_target="tpu_custom_call" | custom-call | tf_op jit(solution)/shard_map/newton_step/pallas_call | solution.py:422
  38.4 1.1 %trade_mix.1 = (f32[16,16,128]{2,1,0:T(8,128)}, f32[128,2,128]{2,1,0:T(2,128)}) custom-call(f32[2,128,128]{2,1,0:T(8,128)S(1)} %get-tuple-element.5.traded, bf16[4,256,256]{2,1,0:T(8,128)(2,1)S(1)} %get-tuple-element.6.mixer, f32[16,16,128]{2,1,0:T(8,128)S(1)} %get-tuple-element.7.costate), custom_call_target="tpu_custom_call" | custom-call | tf_op jit(solution)/shard_map/trade_mix/pallas_call | solution.py:463

commit v7 on v6

--- a/solution.py
+++ b/solution.py
@@ -9,6 +9,12 @@
 
 BLOCKS = 8
 BATCH = 4
+STEPS = (
+    ((2, 2), (2, 1), (1, 2), (2, 3))
+    + ((3, 2), (2, 0), (0, 2), (1, 1))
+    + ((3, 3), (1, 3), (3, 1), (0, 0))
+    + ((1, 0), (0, 1), (3, 0), (0, 3))
+)
 NT = (((1,), (1,)), ((), ()))
 NN = (((1,), (0,)), ((), ()))
 F32 = jnp.float32
@@ -78,15 +84,22 @@
             barrier, inc=1, device_id=(here, lax.rem(zone + step, nreg)), device_id_type=MESH
         )
 
-    swapped = lax.rem(zone, 2) == 1
+    def pick(k, table):
+        found = table[-1]
+        for n, entry in enumerate(table[:-1]):
+            found = jnp.where(k == n, entry, found)
+        return found
+
     at_x, at_y = lax.div(here, BATCH), lax.rem(here, BATCH)
+    own = STEPS.index((0, 0))
+
+    def row_of(k, i):
+        along_x, along_y = [
+            pick(k, [STEPS[n * BATCH + i][axis] for n in range(batches)]) for axis in range(2)
+        ]
+        return lax.rem(at_x + along_x, batches) * BATCH + lax.rem(at_y + along_y, BATCH)
+
     last = nper - 1
-
-    def row_of(k, i):
-        skew = k + lax.div(k, 2) * (1 - 2 * lax.rem(k, 2))
-        other = lax.rem(i + skew, BATCH)
-        along_x, along_y = jnp.where(swapped, other, i), jnp.where(swapped, i, other)
-        return lax.rem(at_x + along_x, batches) * BATCH + lax.rem(at_y + along_y, BATCH)
 
     def load(k, c, i):
         when = pl.ds(per - chunk * (c + 1), chunk)
@@ -135,8 +148,8 @@
 
     def keep_map():
         return [
-            pltpu.make_async_copy(outgoing.at[0], incoming.at[here], map_recv.at[here]),
-            pltpu.make_async_copy(shifts.at[0], given.at[here], shift_recv.at[here]),
+            pltpu.make_async_copy(outgoing.at[own], incoming.at[here], map_recv.at[here]),
+            pltpu.make_async_copy(shifts.at[own], given.at[here], shift_recv.at[here]),
         ]
 
     for copy in small[:2]:
@@ -193,7 +206,7 @@
                 value = jnp.sum(maps[slot, 0] * column, axis=0, keepdims=True)
                 shifts[slot] = value + offsets[slot, 0:1]
 
-        for i in (2, 1, 3, 0):
+        for i in range(BATCH):
             row = row_of(k, i)
 
             @pl.when((row != here) & (here != 0))
@@ -365,11 +378,11 @@
         def _():
             send_edge(row).wait_send()
 
-        @pl.when((row > 0) & (here != 0))
+        @pl.when((row != own) & (here != 0))
         def _():
             move_map(row, here, row)[1].wait_send()
 
-        @pl.when((row > 0) & (here != 0) & (here != last))
+        @pl.when((row != own) & (here != 0) & (here != last))
         def _():
             move_map(row, here, row)[0].wait_send()
 

time: 39.7 us -> 38.4 us (0.967)
  Pallas kernels: 38.9 us -> 37.6 us
    pallas_call x1, Pallas kernels: 37.8 us -> 36.5 us  [shards(): pl.pallas_call(functools.partial(kernel, nper, nreg), out_shape=(pltpu.VM...]
where the time goes in v7:
time: 38.4 us; the launch traced here: 38.2 us
  Pallas kernels  37.6 us (98%)
  between operations  0.64 us (2%)
    pallas_call x1, Pallas kernels, shards(): pl.pallas_call(functools.partial(kernel, nper, nreg), out_shape=(pltpu.VM...  36.5 us
    pallas_call x1, Pallas kernels, shards(): pl.pallas_call(mix, out_shape=(jax.ShapeDtypeStruct((rows, per, sec), F32...  1.12 us

profile of v7, /device:TPU:1, one launch (start us, length us, event | category | flops | bytes accessed | tf_op | source)
XLA Modules:
  0.0 38.2 jit_solution(17923646020565741488)
XLA Ops:
  0.6 36.5 %newton_step.1 = (f32[16,16,128]{2,1,0:T(8,128)S(1)}, f32[2,128,128]{2,1,0:T(8,128)S(1)}, bf16[4,256,256]{2,1,0:T(8,128)(2,1)S(1)}) custom-call(f32[16,16,128,128]{3,2,1,0:T(8,128)} %trans_hbm.1, f32[16,16,128]{2,1,0:T(8,128)} %force_hbm.1, f32[16,128]{1,0:T(8,128)} %term_hbm.1, s32[8,8,128]{2,1,0:T(8,128)} %bitcast.2, f32[8,8,128]{2,1,0:T(8,128)} %bitcast.3), custom_call_target="tpu_custom_call" | custom-call | tf_op jit(solution)/shard_map/newton_step/pallas_call | solution.py:435
  37.1 1.1 %trade_mix.1 = (f32[16,16,128]{2,1,0:T(8,128)}, f32[128,2,128]{2,1,0:T(2,128)}) custom-call(f32[2,128,128]{2,1,0:T(8,128)S(1)} %get-tuple-element.5.traded, bf16[4,256,256]{2,1,0:T(8,128)(2,1)S(1)} %get-tuple-element.6.mixer, f32[16,16,128]{2,1,0:T(8,128)S(1)} %get-tuple-element.7.costate), custom_call_target="tpu_custom_call" | custom-call | tf_op jit(solution)/shard_map/trade_mix/pallas_call | solution.py:476

commit v8 on v7

--- a/solution.py
+++ b/solution.py
@@ -12,8 +12,8 @@
 STEPS = (
     ((2, 2), (2, 1), (1, 2), (2, 3))
     + ((3, 2), (2, 0), (0, 2), (1, 1))
-    + ((3, 3), (1, 3), (3, 1), (0, 0))
-    + ((1, 0), (0, 1), (3, 0), (0, 3))
+    + ((3, 3), (1, 3), (3, 1), (0, 3))
+    + ((0, 1), (1, 0), (3, 0), (0, 0))
 )
 NT = (((1,), (1,)), ((), ()))
 NN = (((1,), (0,)), ((), ()))
@@ -156,15 +156,18 @@
         copy.wait()
 
     def compose(k, carry):
-        @pl.when(k < batches - 1)
-        def _():
-            for c in range(4):
-                for i in range(BATCH):
-                    load(k + 1, c, i).start()
-
         for c in range(4):
             for i in range(BATCH):
                 load(k, c, i).wait()
+
+            if c == 0:
+
+                @pl.when(k < batches - 1)
+                def _():
+                    for later in range(4):
+                        for i in range(BATCH):
+                            load(k + 1, later, i).start()
+
             for inner in range(chunk):
                 t = per - 1 - chunk * c - inner
                 for i in range(BATCH):
@@ -281,6 +284,7 @@
 
     def chain(step, state):
         p = last - 1 - step
+        ship_edge(p)
 
         @pl.when(p != here)
         def _():
@@ -292,7 +296,6 @@
             for copy in keep_map():
                 copy.wait()
 
-        ship_edge(p)
         moved = incoming[p] * upright(state)
         state = jnp.sum(moved, axis=0, keepdims=True) + given[p]
         edges[p - 1] = state

time: 38.4 us -> 38.3 us (level)
  no operation moved by 1% of the time
where the time goes in v8:
time: 38.3 us; the launch traced here: 38.2 us
  Pallas kernels  37.6 us (98%)
  between operations  0.64 us (2%)
    pallas_call x1, Pallas kernels, shards(): pl.pallas_call(functools.partial(kernel, nper, nreg), out_shape=(pltpu.VM...  36.4 us
    pallas_call x1, Pallas kernels, shards(): pl.pallas_call(mix, out_shape=(jax.ShapeDtypeStruct((rows, per, sec), F32...  1.12 us

profile of v8, /device:TPU:1, one launch (start us, length us, event | category | flops | bytes accessed | tf_op | source)
XLA Modules:
  0.0 38.2 jit_solution(784223553479502293)
XLA Ops:
  0.6 36.4 %newton_step.1 = (f32[16,16,128]{2,1,0:T(8,128)S(1)}, f32[2,128,128]{2,1,0:T(8,128)S(1)}, bf16[4,256,256]{2,1,0:T(8,128)(2,1)S(1)}) custom-call(f32[16,16,128,128]{3,2,1,0:T(8,128)} %trans_hbm.1, f32[16,16,128]{2,1,0:T(8,128)} %force_hbm.1, f32[16,128]{1,0:T(8,128)} %term_hbm.1, s32[8,8,128]{2,1,0:T(8,128)} %bitcast.2, f32[8,8,128]{2,1,0:T(8,128)} %bitcast.3), custom_call_target="tpu_custom_call" | custom-call | tf_op jit(solution)/shard_map/newton_step/pallas_call | solution.py:438
  37.1 1.1 %trade_mix.1 = (f32[16,16,128]{2,1,0:T(8,128)}, f32[128,2,128]{2,1,0:T(2,128)}) custom-call(f32[2,128,128]{2,1,0:T(8,128)S(1)} %get-tuple-element.5.traded, bf16[4,256,256]{2,1,0:T(8,128)(2,1)S(1)} %get-tuple-element.6.mixer, f32[16,16,128]{2,1,0:T(8,128)S(1)} %get-tuple-element.7.costate), custom_call_target="tpu_custom_call" | custom-call | tf_op jit(solution)/shard_map/trade_mix/pallas_call | solution.py:479
